TPU v7x, 32 devices: a whole 2x2x4 slice. The times are simulated.
32 devices in a mesh: expert: 8 (over y, x, core), group: 4 (over z).
Axes of the slice: x: 2, y: 2, z: 4, core: 2. Of those that a mesh axis runs over, the one named last changes fastest.
Arguments:
- tokens: bfloat16 [3840, 4096], P('expert', 'group'), may hold values from -6 to 6
- cotangent: bfloat16 [3840, 1024], P('expert'), may hold values from -6 to 6
- routing: int32 [3840, 1], P('expert'), may hold values from 0 to 7; in each aligned block of 480 rows (0 to 479, 480 to 959, ...) at most 120 rows name the same one
- stat_prev: float32 [8, 1024, 1024], P('expert', 'group'), as said below
- root_prev: bfloat16 [8, 1024, 1024], P('expert', 'group'), may hold values from -0.1875 to 0.1875
- owner_map: int32 [8], replicated, may hold values from 0 to 2, as said below
Outputs:
- statistic: float32 [8, 1024, 1024], P('expert', 'group')
- roots: bfloat16 [8, 1024, 1024], P('expert', 'group')
- update: bfloat16 [8, 4096, 1024], P('expert', 'group')
Inputs may be any that keep to these rules, and one draw needn't show every extreme that they name: `routing`: in the rows of one device (aligned blocks of 480 rows) no expert is named more than 120 times, a bound that some block reaches. `owner_map`: A value below 2 names the index of expert that owns this expert's statistic; the value 2 marks a statistic that is not refreshed. Exactly 4 experts are refreshed; no owner holds more than 4 of them, and some owner holds exactly 4. `stat_prev`: each expert's block is symmetric and positive definite.
All inputs are finite; a program needn't handle non-finite values.
Results may differ from a plain program's by a relative error of at most 0.0055.
Values may be sent and summed in bfloat16 or wider, within the bound.
A program may use at most 64 MiB of HBM per device.

v0:
```python
import functools
import math

import jax
import jax.numpy as jnp
from jax import lax
from jax.experimental import pallas as pl
from jax.experimental.pallas import tpu as pltpu
from jax.sharding import PartitionSpec as P

ITERS = 2
POWER = 8
MESH = pl.DeviceIdType.MESH

keep_share = 0.9


def exchange_kernel(
    experts, groups, tok_ref, sig_ref, pay_ref, got_tok, got_sig, full,
    hold_tok, hold_sig, hold_pay, tok_send, tok_recv, sig_send, sig_recv, pay_send, pay_recv, own_sem,
):
    me = lax.axis_index("expert")
    mine = lax.axis_index("group")
    barrier = pltpu.get_barrier_semaphore()
    for d in range(1, experts):
        pl.semaphore_signal(
            barrier, inc=1, device_id={"expert": lax.rem(me + d, experts)}, device_id_type=MESH
        )
    for d in range(1, groups):
        pl.semaphore_signal(
            barrier, inc=1, device_id={"group": lax.rem(mine + d, groups)}, device_id_type=MESH
        )
    pl.semaphore_wait(barrier, experts + groups - 2)
    copies = []
    for d in range(1, max(experts, groups)):
        if d < groups:
            copies.append(
                pltpu.make_async_remote_copy(
                    src_ref=pay_ref,
                    dst_ref=full.at[mine],
                    send_sem=pay_send.at[d],
                    recv_sem=pay_recv.at[d],
                    device_id={"group": lax.rem(mine + d, groups)},
                    device_id_type=MESH,
                )
            )
        if d < experts:
            peer = lax.rem(me + d, experts)
            for src, dst, ssem, rsem in (
                (tok_ref, got_tok, tok_send, tok_recv),
                (sig_ref, got_sig, sig_send, sig_recv),
            ):
                copies.append(
                    pltpu.make_async_remote_copy(
                        src_ref=src.at[peer],
                        dst_ref=dst.at[me],
                        send_sem=ssem.at[d],
                        recv_sem=rsem.at[d],
                        device_id={"expert": peer},
                        device_id_type=MESH,
                    )
                )
    for copy in copies:
        copy.start()
    inward = (
        pltpu.make_async_copy(tok_ref.at[me], hold_tok, own_sem.at[0]),
        pltpu.make_async_copy(sig_ref.at[me], hold_sig, own_sem.at[1]),
        pltpu.make_async_copy(pay_ref, hold_pay, own_sem.at[2]),
    )
    for copy in inward:
        copy.start()
    for copy in inward:
        copy.wait()
    outward = (
        pltpu.make_async_copy(hold_tok, got_tok.at[me], own_sem.at[3]),
        pltpu.make_async_copy(hold_sig, got_sig.at[me], own_sem.at[4]),
        pltpu.make_async_copy(hold_pay, full.at[mine], own_sem.at[5]),
    )
    for copy in outward:
        copy.start()
    for copy in outward:
        copy.wait()
    for copy in copies:
        copy.wait()


def exchange(send_tokens, send_signal, payload, experts, groups):
    anywhere = pl.BlockSpec(memory_space=pl.ANY)
    dma = pltpu.SemaphoreType.DMA
    return pl.pallas_call(
        functools.partial(exchange_kernel, experts, groups),
        out_shape=(
            jax.ShapeDtypeStruct(send_tokens.shape, send_tokens.dtype),
            jax.ShapeDtypeStruct(send_signal.shape, send_signal.dtype),
            jax.ShapeDtypeStruct((groups,) + payload.shape, payload.dtype),
        ),
        in_specs=[anywhere] * 3,
        out_specs=(anywhere,) * 3,
        scratch_shapes=[
            pltpu.VMEM(send_tokens.shape[1:], send_tokens.dtype),
            pltpu.VMEM(send_signal.shape[1:], send_signal.dtype),
            pltpu.VMEM(payload.shape, payload.dtype),
            dma((experts,)), dma((experts,)), dma((experts,)), dma((experts,)),
            dma((groups,)), dma((groups,)), dma((6,)),
        ],
        compiler_params=pltpu.CompilerParams(collective_id=0, has_side_effects=True),
    )(send_tokens, send_signal, payload)


def chain_kernel(
    groups, share, part_ref, full_ref, prev_ref, low_ref, stat_ref,
    from_left, from_right, to_right, to_left, right_send, right_recv, left_send, left_recv,
):
    mine = lax.axis_index("group")
    last = groups - 1
    side = part_ref.shape[1]
    barrier = pltpu.get_barrier_semaphore()

    for shift in (1, last):
        pl.semaphore_signal(
            barrier, inc=1, device_id={"group": lax.rem(mine + shift, groups)}, device_id_type=MESH
        )
    pl.semaphore_wait(barrier, 2)

    def rightward(k, src):
        return pltpu.make_async_remote_copy(
            src_ref=src.at[k],
            dst_ref=from_left.at[k],
            send_sem=right_send.at[k],
            recv_sem=right_recv.at[k],
            device_id={"group": lax.rem(mine + 1, groups)},
            device_id_type=MESH,
        )

    def leftward(k, src):
        return pltpu.make_async_remote_copy(
            src_ref=src.at[k],
            dst_ref=from_right.at[k],
            send_sem=left_send.at[k],
            recv_sem=left_recv.at[k],
            device_id={"group": lax.rem(mine + last, groups)},
            device_id_type=MESH,
        )

    pairs = [(r, c) for r in range(groups) for c in range(r, groups)]

    @pl.when(mine == 0)
    def _():
        for k in range(len(pairs)):
            rightward(k, part_ref).start()

    @pl.when(mine == last)
    def _():
        for k in range(len(pairs)):
            leftward(k, part_ref).start()

    def emit(k, total):
        r, c = pairs[k]
        rows, columns = slice(r * side, (r + 1) * side), slice(c * side, (c + 1) * side)
        scaled = share * total
        low = keep_share * full_ref[r, :, columns].astype(jnp.float32) + scaled
        low_ref[rows, columns] = low.astype(jnp.bfloat16)

        @pl.when(mine == r)
        def _():
            stat_ref[:, columns] = keep_share * prev_ref[:, columns] + scaled

        if c > r:
            low_ref[columns, rows] = low.T.astype(jnp.bfloat16)

            @pl.when(mine == c)
            def _():
                stat_ref[:, rows] = keep_share * prev_ref[:, rows] + scaled.T

    def own(k):
        return part_ref[k].astype(jnp.float32)

    def pass_right(k):
        rightward(k, to_right).wait_recv()
        to_right[k] = (own(k) + from_left[k].astype(jnp.float32)).astype(jnp.bfloat16)
        rightward(k, to_right).start()

    def pass_left(k):
        leftward(k, to_left).wait_recv()
        to_left[k] = (own(k) + from_right[k].astype(jnp.float32)).astype(jnp.bfloat16)
        leftward(k, to_left).start()

    def finish(k):
        emit(k, own(k) + from_left[k].astype(jnp.float32) + from_right[k].astype(jnp.float32))

    count = len(pairs)

    @pl.when(mine == 0)
    def _():
        for k in range(count):
            leftward(k, to_left).wait_recv()
            emit(k, own(k) + from_right[k].astype(jnp.float32))

    @pl.when(mine == last)
    def _():
        for k in range(count):
            rightward(k, to_right).wait_recv()
            emit(k, own(k) + from_left[k].astype(jnp.float32))

    lag = 2
    for near, far, here in (
        (pass_right, pass_left, (mine > 0) & (2 * mine < last)),
        (pass_left, pass_right, (mine < last) & (2 * mine >= last)),
    ):

        @pl.when(here)
        def _():
            for step in range(count + lag):
                if step < count:
                    near(step)
                if step >= lag:
                    far(step - lag)
                    finish(step - lag)

    for k in range(count):

        @pl.when(mine < last)
        def _():
            rightward(k, to_right).wait_send()

        @pl.when(mine > 0)
        def _():
            leftward(k, to_left).wait_send()


def chain_sum(part, full, prev_rows, share, groups):
    count, side = part.shape[0], part.shape[1]
    vmem = pl.BlockSpec(memory_space=pltpu.VMEM)
    dma = pltpu.SemaphoreType.DMA
    return pl.pallas_call(
        functools.partial(chain_kernel, groups, share),
        out_shape=(
            jax.ShapeDtypeStruct((groups * side, groups * side), jnp.bfloat16),
            jax.ShapeDtypeStruct(prev_rows.shape, jnp.float32),
        ),
        in_specs=[vmem] * 3,
        out_specs=(vmem, vmem),
        scratch_shapes=[pltpu.VMEM(part.shape, part.dtype)] * 4 + [dma((count,))] * 4,
        compiler_params=pltpu.CompilerParams(
            collective_id=1, has_side_effects=True, vmem_limit_bytes=40 << 20
        ),
    )(part, full, prev_rows)


def root_kernel(
    groups, live_ref, low_ref, full_hbm, grad_hbm, rows_ref, update_hbm,
    grad_ref, factor, moment, square, fourth, root, result, sems,
):
    mine = lax.axis_index("group")
    order = low_ref.shape[0]
    side = order // groups
    fetch = pltpu.make_async_copy(grad_hbm, grad_ref, sems.at[0])
    fetch.start()
    live = live_ref[0] == 1

    @pl.when(live)
    def _():
        vector = jnp.full((16, order), 1.0 / math.sqrt(order), jnp.float32)
        length = jnp.ones((1, 1), jnp.float32)
        for turn_index in range(POWER):
            image = jnp.dot(
                vector.astype(jnp.bfloat16), low_ref[...], preferred_element_type=jnp.float32
            )
            first = image[:1]
            length = jnp.sqrt(jnp.sum(first * first, axis=1, keepdims=True))
            vector = image / length
        scaling = 2.5 / length
        outer = jnp.sqrt(jnp.sqrt(scaling))

        def tile(t):
            return pl.ds(pl.multiple_of(t * side, side), side)

        def factor_of(t, value):
            row = lax.broadcasted_iota(jnp.int32, (side, order), 0) + t * side
            column = lax.broadcasted_iota(jnp.int32, (side, order), 1)
            identity = (row == column).astype(jnp.float32)
            return ((5.0 * identity - value) * 0.25).astype(jnp.bfloat16)

        def product(left, right, t):
            return jnp.dot(left[tile(t), :], right[...], preferred_element_type=jnp.float32)

        @pl.loop(0, groups)
        def _(t):
            value = scaling * low_ref[tile(t), :].astype(jnp.float32)
            moment[tile(t), :] = value.astype(jnp.bfloat16)
            factor[tile(t), :] = factor_of(t, value)

        @pl.loop(0, groups)
        def _(t):
            square[tile(t), :] = product(factor, factor, t).astype(jnp.bfloat16)

        @pl.loop(0, groups)
        def _(t):
            fourth[tile(t), :] = product(square, square, t).astype(jnp.bfloat16)

        @pl.loop(0, groups)
        def _(t):
            root[tile(t), :] = factor_of(t, product(fourth, moment, t))

        @pl.loop(0, groups)
        def _(t):
            square[tile(t), :] = (outer * product(factor, root, t)).astype(jnp.bfloat16)

    @pl.when(jnp.logical_not(live))
    def _():
        prior = pltpu.make_async_copy(full_hbm, square, sems.at[1])
        prior.start()
        prior.wait()

    rows_ref[...] = square[pl.ds(pl.multiple_of(mine * side, side), side), :]
    fetch.wait()
    tall = grad_ref.shape[0] // groups
    sends = []
    for t in range(groups):
        part = slice(t * tall, (t + 1) * tall)
        result[part, :] = jnp.dot(
            grad_ref[part, :], square[...], preferred_element_type=jnp.float32
        ).astype(jnp.bfloat16)
        sends.append(
            pltpu.make_async_copy(result.at[part, :], update_hbm.at[part, :], sems.at[2 + t])
        )
        sends[-1].start()
    for send in sends:
        send.wait()


def finish_roots(live, low, full, grad, groups):
    order = low.shape[0]
    vmem = pl.BlockSpec(memory_space=pltpu.VMEM)
    anywhere = pl.BlockSpec(memory_space=pl.ANY)
    square = pltpu.VMEM((order, order), jnp.bfloat16)
    tall = pltpu.VMEM(grad.shape, jnp.bfloat16)
    return pl.pallas_call(
        functools.partial(root_kernel, groups),
        out_shape=(
            jax.ShapeDtypeStruct((order // groups, order), jnp.bfloat16),
            jax.ShapeDtypeStruct(grad.shape, jnp.bfloat16),
        ),
        in_specs=[pl.BlockSpec(memory_space=pltpu.SMEM), vmem, anywhere, anywhere],
        out_specs=(vmem, anywhere),
        scratch_shapes=[
            tall, square, square, square, square, square, tall,
            pltpu.SemaphoreType.DMA((2 + groups,)),
        ],
        compiler_params=pltpu.CompilerParams(vmem_limit_bytes=40 << 20),
    )(live, low, full, grad)


def body(tokens, cotangent, routing, stat_prev, root_prev, owner_map):
    expert_count = lax.axis_size("expert")
    group_count = lax.axis_size("group")
    my_expert = lax.axis_index("expert")
    my_group = lax.axis_index("group")
    tok_rows = tokens.shape[0]
    width_part = tokens.shape[1]
    hidden = cotangent.shape[1]
    row_block = stat_prev.shape[1]
    capacity = 2 * tok_rows // expert_count
    owners = expert_count // 4
    route = routing[:, 0]
    order = jnp.arange(tok_rows, dtype=jnp.int32)
    earlier = (route[:, None] == route[None, :]) & (order[:, None] < order[None, :])
    position = jnp.sum(earlier.astype(jnp.int32), axis=0)
    column = route * capacity + position
    slots = jnp.arange(expert_count * capacity, dtype=jnp.int32)
    select = (slots[:, None] == column[None, :]).astype(jnp.bfloat16)
    send_tokens = jnp.dot(select, tokens, preferred_element_type=jnp.float32)
    send_tokens = send_tokens.astype(jnp.bfloat16).reshape(expert_count, capacity, width_part)
    send_signal = jnp.dot(select, cotangent, preferred_element_type=jnp.float32)
    send_signal = send_signal.astype(jnp.bfloat16).reshape(expert_count, capacity, hidden)
    my_live = jnp.take(owner_map, my_expert) < owners
    payload = jnp.where(my_live, stat_prev[0].astype(jnp.bfloat16), root_prev[0])
    got_tokens, got_signal, full = exchange(
        send_tokens, send_signal, payload, expert_count, group_count
    )
    got_tokens = got_tokens.reshape(expert_count * capacity, width_part)
    got_signal = got_signal.reshape(expert_count * capacity, hidden)
    grad = lax.dot_general(
        got_tokens, got_signal, (((0,), (0,)), ((), ())), preferred_element_type=jnp.float32
    )
    grad = (grad * (1.0 / math.sqrt(tok_rows))).astype(jnp.bfloat16)
    parts = []
    for r in range(group_count):
        panel = lax.dot_general(
            grad[:, r * row_block : (r + 1) * row_block],
            grad[:, r * row_block :],
            (((0,), (0,)), ((), ())),
            preferred_element_type=jnp.float32,
        ).astype(jnp.bfloat16)
        for c in range(group_count - r):
            parts.append(panel[:, c * row_block : (c + 1) * row_block])
    share = (1.0 - keep_share) / (width_part * group_count)
    stat_low, stat_new = chain_sum(jnp.stack(parts), full, stat_prev[0], share, group_count)
    live_flag = my_live.astype(jnp.int32).reshape(1)
    root_rows, update = finish_roots(
        live_flag, stat_low, full.reshape(hidden, hidden), grad, group_count
    )
    return (stat_new[None], root_rows[None], update[None])


def solution(mesh):
    in_specs = (
        P("expert", "group"),
        P("expert", None),
        P("expert", None),
        P("expert", "group", None),
        P("expert", "group", None),
        P(),
    )
    out_specs = (P("expert", "group", None), P("expert", "group", None), P("expert", "group", None))
    return jax.shard_map(body, mesh=mesh, in_specs=in_specs, out_specs=out_specs, check_vma=False)
```

profile of v0, /device:TPU:1, one launch (start us, length us, event | category | flops | bytes accessed | tf_op | source)
XLA Modules:
  0.0 133.2 jit_solution(12992878295045578367)
XLA Ops:
  0.6 0.0 copy-start
  0.7 1.3 dynamic-slice.2
  2.6 0.9 convert_reduce_fusion
  3.6 0.7 multiply_add_fusion
  4.2 2.3 %bitcast_select_fusion.pay_ref = bf16[256,1024]{1,0:T(8,128)(2,1)} fusion(bf16[1,256,1024]{2,1,0:T(8,128)(2,1)} %param.10, pred[]{:T(512)} %bitcast.4, f32[1,256,1024]{2,1,0:T(8,128)} %param.9), kind=kLoop, calls=%fused_computation.25 | loop fusion | flops 524288 | bytes 2097153 | tf_op jit(solution)/shard_map/jit(_where)/select_n | solution.py:377
  6.5 0.0 copy-done
  6.5 0.0 copy-start.3
  6.5 2.4 %fusion.4 = bf16[960,1024]{1,0:T(8,128)(2,1)} fusion(bf16[480,1024]{1,0:T(8,128)(2,1)S(1)} %copy-done, s32[480]{0:T(512)S(1)} %multiply_add_fusion), kind=kOutput, calls=%fused_computation.6 | convolution fusion | flops 945162240 | bytes 2951040 | tf_op jit(solution)/shard_map/dot_general | solution.py:374
  8.9 0.0 copy-done.3
  8.9 2.5 %fusion.3 = bf16[960,1024]{1,0:T(8,128)(2,1)} fusion(bf16[480,1024]{1,0:T(8,128)(2,1)S(1)} %copy-done.3, s32[480]{0:T(512)S(1)} %multiply_add_fusion), kind=kOutput, calls=%fused_computation.5 | convolution fusion | flops 945162240 | bytes 2951040 | tf_op jit(solution)/shard_map/dot_general | solution.py:372
  11.4 49.2 %shard_map.85 = (bf16[8,120,1024]{2,1,0:T(8,128)(2,1)}, bf16[8,120,1024]{2,1,0:T(8,128)(2,1)}, bf16[4,256,1024]{2,1,0:T(8,128)(2,1)}) custom-call(bf16[8,120,1024]{2,1,0:T(8,128)(2,1)} %bitcast.67, bf16[8,120,1024]{2,1,0:T(8,128)(2,1)} %bitcast.66, bf16[256,1024]{1,0:T(8,128)(2,1)} %bitcast_select_fusion.pay_ref), custom_call_target="tpu_custom_call" | custom-call | tf_op jit(solution)/shard_map/pallas_call | solution.py:90
  60.6 4.5 %fusion.grad_hbm = bf16[1024,1024]{1,0:T(8,128)(2,1)S(1)} fusion(bf16[8,120,1024]{2,1,0:T(8,128)(2,1)} %get-tuple-element.10, bf16[8,120,1024]{2,1,0:T(8,128)(2,1)} %get-tuple-element.11), kind=kOutput, calls=%fused_computation.1 | convolution fusion | flops 2015363072 | bytes 6029312 | tf_op jit(solution)/shard_map/dot_general | solution.py:383
  65.1 0.5 convolution_convert_fusion.1
  65.6 0.6 fusion.7
  66.2 0.7 convolution_convert_fusion
  67.0 0.0 copy-start.1
  67.0 0.0 copy-start.2
  67.2 0.4 fusion.11.part_ref
  67.6 1.0 copy-done.1
  68.6 0.3 copy-done.2
  68.8 42.7 %shard_map.86 = (bf16[1024,1024]{1,0:T(8,128)(2,1)S(1)}, f32[256,1024]{1,0:T(8,128)S(1)}) custom-call(bf16[10,256,256]{2,1,0:T(8,128)(2,1)S(1)} %fusion.11.part_ref, bf16[4,256,1024]{2,1,0:T(8,128)(2,1)S(1)} %copy-done.1, f32[256,1024]{1,0:T(8,128)S(1)} %bitcast.64), custom_call_target="tpu_custom_call" | custom-call | tf_op jit(solution)/shard_map/pallas_call | solution.py:235
  111.6 20.6 %shard_map.87 = (bf16[256,1024]{1,0:T(8,128)(2,1)}, bf16[1024,1024]{1,0:T(8,128)(2,1)}) custom-call(s32[1]{0:T(128)} %bitcast.19.live_ref, bf16[1024,1024]{1,0:T(8,128)(2,1)S(1)} %get-tuple-element.14.low_ref, bf16[1024,1024]{1,0:T(8,128)(2,1)S(1)} %bitcast.63, bf16[1024,1024]{1,0:T(8,128)(2,1)S(1)} %fusion.grad_hbm), custom_call_target="tpu_custom_call" | custom-call | tf_op jit(solution)/shard_map/pallas_call | solution.py:338
  132.2 1.0 copy.19
  (9 shorter events, 0.1 us)
Async XLA Ops:
  0.6 5.9 %copy-start = (bf16[480,1024]{1,0:T(8,128)(2,1)S(1)}, bf16[480,1024]{1,0:T(8,128)(2,1)}, u32[]{:S(2)}) copy-start(bf16[480,1024]{1,0:T(8,128)(2,1)} %param.7) | copy-start | bytes 2949124
  6.5 2.4 %copy-start.3 = (bf16[480,1024]{1,0:T(8,128)(2,1)S(1)}, bf16[480,1024]{1,0:T(8,128)(2,1)}, u32[]{:S(2)}) copy-start(bf16[480,1024]{1,0:T(8,128)(2,1)} %param.6) | copy-start | bytes 2949124
  67.0 1.6 %copy-start.1 = (bf16[4,256,1024]{2,1,0:T(8,128)(2,1)S(1)}, bf16[4,256,1024]{2,1,0:T(8,128)(2,1)}, u32[]{:S(2)}) copy-start(bf16[4,256,1024]{2,1,0:T(8,128)(2,1)} %get-tuple-element.12.full_ref) | copy-start | bytes 6291460
  67.0 1.8 %copy-start.2 = (f32[1,256,1024]{2,1,0:T(8,128)S(1)}, f32[1,256,1024]{2,1,0:T(8,128)}, u32[]{:S(2)}) copy-start(f32[1,256,1024]{2,1,0:T(8,128)} %param.9) | copy-start | bytes 3145732
where the time goes:
time: 135 us; the launch traced here: 133 us
  Pallas kernels  113 us (84%)
  matrix products  11.6 us (9%)
  other arithmetic  3.87 us (3%)
  local copies, waits for them, and re-layouts  3.71 us (3%)
  between operations  1.45 us (1%)
    pallas_call x1, Pallas kernels, exchange(): pl.pallas_call(functools.partial(exchange_kernel, experts, groups), out_s...  49.2 us
    pallas_call x1, Pallas kernels, chain_sum(): pl.pallas_call(functools.partial(chain_kernel, groups, share), out_shape=...  42.7 us
    pallas_call x1, Pallas kernels, finish_roots(): pl.pallas_call(functools.partial(root_kernel, groups), out_shape=(jax.Sha...  20.6 us
    dot_general x1, matrix products, body(): lax.dot_general(got_tokens, got_signal, (((0,), (0,)), ((), ())), preferr...  4.52 us

commit v1 on v0

--- a/solution.py
+++ b/solution.py
@@ -13,6 +13,60 @@
 MESH = pl.DeviceIdType.MESH
 
 keep_share = 0.9
+
+
+def prepare_kernel(
+    capacity, owners, pieces, owner_ref, tall_ref, wide_ref, tok_ref, sig_ref, prev_ref, old_ref,
+    tok_hbm, sig_hbm, pay_hbm, tok_out, sig_out, pay_out, sems,
+):
+    tok_rows = tok_ref.shape[0]
+    live = owner_ref[lax.axis_index("expert")] < owners
+    pay_out[...] = jnp.where(live, prev_ref[...].astype(jnp.bfloat16), old_ref[...])
+    sends = [pltpu.make_async_copy(pay_out, pay_hbm, sems.at[2 * pieces])]
+    sends[0].start()
+    wide = wide_ref[...]
+    before = lax.broadcasted_iota(jnp.int32, (tok_rows, tok_rows), 0)
+    after = lax.broadcasted_iota(jnp.int32, (tok_rows, tok_rows), 1)
+    earlier = jnp.where((tall_ref[...] == wide) & (before < after), 1, 0)
+    column = wide * capacity + jnp.sum(earlier, axis=0, keepdims=True)
+    piece = tok_out.shape[0] // pieces
+    for t in range(pieces):
+        rows = slice(t * piece, (t + 1) * piece)
+        slots = lax.broadcasted_iota(jnp.int32, (piece, tok_rows), 0) + t * piece
+        select = (slots == column).astype(jnp.float32).astype(jnp.bfloat16)
+        for which, (src, out, hbm) in enumerate(
+            ((tok_ref, tok_out, tok_hbm), (sig_ref, sig_out, sig_hbm))
+        ):
+            out[rows, :] = jnp.dot(
+                select, src[...], preferred_element_type=jnp.float32
+            ).astype(jnp.bfloat16)
+            sends.append(
+                pltpu.make_async_copy(
+                    out.at[rows, :], hbm.at[rows, :], sems.at[2 * t + which]
+                )
+            )
+            sends[-1].start()
+    for send in sends:
+        send.wait()
+
+
+def prepare(owner_map, routing, tokens, cotangent, prev_rows, old_rows, experts, capacity, owners):
+    slots = experts * capacity
+    pieces = 4 if slots % 64 == 0 else 1
+    vmem = pl.BlockSpec(memory_space=pltpu.VMEM)
+    anywhere = pl.BlockSpec(memory_space=pl.ANY)
+    shapes = (
+        (slots, tokens.shape[1]), (slots, cotangent.shape[1]), prev_rows.shape,
+    )
+    return pl.pallas_call(
+        functools.partial(prepare_kernel, capacity, owners, pieces),
+        out_shape=tuple(jax.ShapeDtypeStruct(shape, jnp.bfloat16) for shape in shapes),
+        in_specs=[pl.BlockSpec(memory_space=pltpu.SMEM)] + [vmem] * 6,
+        out_specs=(anywhere,) * 3,
+        scratch_shapes=[pltpu.VMEM(shape, jnp.bfloat16) for shape in shapes]
+        + [pltpu.SemaphoreType.DMA((2 * pieces + 1,))],
+        compiler_params=pltpu.CompilerParams(vmem_limit_bytes=40 << 20),
+    )(owner_map, routing, routing.reshape(1, -1), tokens, cotangent, prev_rows, old_rows)
 
 
 def exchange_kernel(
@@ -26,40 +80,49 @@
         pl.semaphore_signal(
             barrier, inc=1, device_id={"expert": lax.rem(me + d, experts)}, device_id_type=MESH
         )
-    for d in range(1, groups):
+    for d in (1, groups - 1):
         pl.semaphore_signal(
             barrier, inc=1, device_id={"group": lax.rem(mine + d, groups)}, device_id_type=MESH
         )
-    pl.semaphore_wait(barrier, experts + groups - 2)
+    pl.semaphore_wait(barrier, experts + 1)
+    last = groups - 1
+
+    def relay(d, step, src):
+        origin = lax.rem(mine + (groups - d) * step, groups)
+        return pltpu.make_async_remote_copy(
+            src_ref=full.at[origin] if src is None else src,
+            dst_ref=full.at[origin],
+            send_sem=pay_send.at[0 if d == 1 else 1, step],
+            recv_sem=pay_recv.at[0 if d == 1 else 1, step],
+            device_id={"group": lax.rem(mine + d, groups)},
+            device_id_type=MESH,
+        )
+
+    @pl.when(mine < last)
+    def _():
+        relay(1, 0, pay_ref).start()
+
+    @pl.when(mine > 0)
+    def _():
+        relay(last, 0, pay_ref).start()
+
     copies = []
-    for d in range(1, max(experts, groups)):
-        if d < groups:
+    for d in range(1, experts):
+        peer = lax.rem(me + d, experts)
+        for src, dst, ssem, rsem in (
+            (tok_ref, got_tok, tok_send, tok_recv),
+            (sig_ref, got_sig, sig_send, sig_recv),
+        ):
             copies.append(
                 pltpu.make_async_remote_copy(
-                    src_ref=pay_ref,
-                    dst_ref=full.at[mine],
-                    send_sem=pay_send.at[d],
-                    recv_sem=pay_recv.at[d],
-                    device_id={"group": lax.rem(mine + d, groups)},
+                    src_ref=src.at[peer],
+                    dst_ref=dst.at[me],
+                    send_sem=ssem.at[d],
+                    recv_sem=rsem.at[d],
+                    device_id={"expert": peer},
                     device_id_type=MESH,
                 )
             )
-        if d < experts:
-            peer = lax.rem(me + d, experts)
-            for src, dst, ssem, rsem in (
-                (tok_ref, got_tok, tok_send, tok_recv),
-                (sig_ref, got_sig, sig_send, sig_recv),
-            ):
-                copies.append(
-                    pltpu.make_async_remote_copy(
-                        src_ref=src.at[peer],
-                        dst_ref=dst.at[me],
-                        send_sem=ssem.at[d],
-                        recv_sem=rsem.at[d],
-                        device_id={"expert": peer},
-                        device_id_type=MESH,
-                    )
-                )
     for copy in copies:
         copy.start()
     inward = (
@@ -80,6 +143,34 @@
         copy.start()
     for copy in outward:
         copy.wait()
+    for step in range(last):
+
+        @pl.when(mine > step)
+        def _():
+            relay(1, step, None).wait_recv()
+
+        @pl.when((mine > step) & (mine < last))
+        def _():
+            relay(1, step + 1, None).start()
+
+        @pl.when(last - mine > step)
+        def _():
+            relay(last, step, None).wait_recv()
+
+        @pl.when((last - mine > step) & (mine > 0))
+        def _():
+            relay(last, step + 1, None).start()
+
+    for step in range(groups):
+
+        @pl.when((mine >= step) & (mine < last))
+        def _():
+            relay(1, step, None).wait_send()
+
+        @pl.when((last - mine >= step) & (mine > 0))
+        def _():
+            relay(last, step, None).wait_send()
+
     for copy in copies:
         copy.wait()
 
@@ -101,7 +192,7 @@
             pltpu.VMEM(send_signal.shape[1:], send_signal.dtype),
             pltpu.VMEM(payload.shape, payload.dtype),
             dma((experts,)), dma((experts,)), dma((experts,)), dma((experts,)),
-            dma((groups,)), dma((groups,)), dma((6,)),
+            dma((2, groups)), dma((2, groups)), dma((6,)),
         ],
         compiler_params=pltpu.CompilerParams(collective_id=0, has_side_effects=True),
     )(send_tokens, send_signal, payload)
@@ -248,15 +339,20 @@
 
 
 def root_kernel(
-    groups, live_ref, low_ref, full_hbm, grad_hbm, rows_ref, update_hbm,
-    grad_ref, factor, moment, square, fourth, root, result, sems,
+    groups, owners, owner_ref, low_ref, full_hbm, grad_hbm, stat_hbm, rows_ref, update_hbm, new_hbm,
+    stat_ref, grad_ref, factor, moment, square, fourth, root, result, sems,
 ):
     mine = lax.axis_index("group")
     order = low_ref.shape[0]
     side = order // groups
     fetch = pltpu.make_async_copy(grad_hbm, grad_ref, sems.at[0])
     fetch.start()
-    live = live_ref[0] == 1
+    take = pltpu.make_async_copy(stat_hbm, stat_ref, sems.at[2 + groups])
+    take.start()
+    live = owner_ref[lax.axis_index("expert")] < owners
+    take.wait()
+    give = pltpu.make_async_copy(stat_ref, new_hbm, sems.at[3 + groups])
+    give.start()
 
     @pl.when(live)
     def _():
@@ -327,54 +423,47 @@
         sends[-1].start()
     for send in sends:
         send.wait()
-
-
-def finish_roots(live, low, full, grad, groups):
+    give.wait()
+
+
+def finish_roots(owner_map, low, full, grad, stat, groups, owners):
     order = low.shape[0]
     vmem = pl.BlockSpec(memory_space=pltpu.VMEM)
     anywhere = pl.BlockSpec(memory_space=pl.ANY)
     square = pltpu.VMEM((order, order), jnp.bfloat16)
     tall = pltpu.VMEM(grad.shape, jnp.bfloat16)
     return pl.pallas_call(
-        functools.partial(root_kernel, groups),
+        functools.partial(root_kernel, groups, owners),
         out_shape=(
             jax.ShapeDtypeStruct((order // groups, order), jnp.bfloat16),
             jax.ShapeDtypeStruct(grad.shape, jnp.bfloat16),
+            jax.ShapeDtypeStruct(stat.shape, jnp.float32),
         ),
-        in_specs=[pl.BlockSpec(memory_space=pltpu.SMEM), vmem, anywhere, anywhere],
-        out_specs=(vmem, anywhere),
+        in_specs=[pl.BlockSpec(memory_space=pltpu.SMEM), vmem] + [anywhere] * 3,
+        out_specs=(vmem, anywhere, anywhere),
         scratch_shapes=[
-            tall, square, square, square, square, square, tall,
-            pltpu.SemaphoreType.DMA((2 + groups,)),
+            pltpu.VMEM(stat.shape, jnp.float32), tall, square, square, square, square, square, tall,
+            pltpu.SemaphoreType.DMA((4 + groups,)),
         ],
         compiler_params=pltpu.CompilerParams(vmem_limit_bytes=40 << 20),
-    )(live, low, full, grad)
+    )(owner_map, low, full, grad, stat)
 
 
 def body(tokens, cotangent, routing, stat_prev, root_prev, owner_map):
     expert_count = lax.axis_size("expert")
     group_count = lax.axis_size("group")
-    my_expert = lax.axis_index("expert")
-    my_group = lax.axis_index("group")
     tok_rows = tokens.shape[0]
     width_part = tokens.shape[1]
     hidden = cotangent.shape[1]
     row_block = stat_prev.shape[1]
     capacity = 2 * tok_rows // expert_count
     owners = expert_count // 4
-    route = routing[:, 0]
-    order = jnp.arange(tok_rows, dtype=jnp.int32)
-    earlier = (route[:, None] == route[None, :]) & (order[:, None] < order[None, :])
-    position = jnp.sum(earlier.astype(jnp.int32), axis=0)
-    column = route * capacity + position
-    slots = jnp.arange(expert_count * capacity, dtype=jnp.int32)
-    select = (slots[:, None] == column[None, :]).astype(jnp.bfloat16)
-    send_tokens = jnp.dot(select, tokens, preferred_element_type=jnp.float32)
-    send_tokens = send_tokens.astype(jnp.bfloat16).reshape(expert_count, capacity, width_part)
-    send_signal = jnp.dot(select, cotangent, preferred_element_type=jnp.float32)
-    send_signal = send_signal.astype(jnp.bfloat16).reshape(expert_count, capacity, hidden)
-    my_live = jnp.take(owner_map, my_expert) < owners
-    payload = jnp.where(my_live, stat_prev[0].astype(jnp.bfloat16), root_prev[0])
+    send_tokens, send_signal, payload = prepare(
+        owner_map, routing, tokens, cotangent, stat_prev[0], root_prev[0],
+        expert_count, capacity, owners,
+    )
+    send_tokens = send_tokens.reshape(expert_count, capacity, width_part)
+    send_signal = send_signal.reshape(expert_count, capacity, hidden)
     got_tokens, got_signal, full = exchange(
         send_tokens, send_signal, payload, expert_count, group_count
     )
@@ -396,9 +485,8 @@
             parts.append(panel[:, c * row_block : (c + 1) * row_block])
     share = (1.0 - keep_share) / (width_part * group_count)
     stat_low, stat_new = chain_sum(jnp.stack(parts), full, stat_prev[0], share, group_count)
-    live_flag = my_live.astype(jnp.int32).reshape(1)
-    root_rows, update = finish_roots(
-        live_flag, stat_low, full.reshape(hidden, hidden), grad, group_count
+    root_rows, update, stat_new = finish_roots(
+        owner_map, stat_low, full.reshape(hidden, hidden), grad, stat_new, group_count, owners
     )
     return (stat_new[None], root_rows[None], update[None])
 

time: 135 us -> 140 us (1.037)
  the two profiles are of different devices: /device:TPU:1 before, /device:TPU:0 now
where the time goes in v1:
time: 140 us
  Pallas kernels  121 us (86%)
  local copies, waits for them, and re-layouts  11.6 us (8%)
  matrix products  6.68 us (5%)
    pallas_call x1, Pallas kernels, exchange(): pl.pallas_call(functools.partial(exchange_kernel, experts, groups), out_s...  48 us
    pallas_call x1, Pallas kernels, chain_sum(): pl.pallas_call(functools.partial(chain_kernel, groups, share), out_shape=...  44.5 us
    pallas_call x1, Pallas kernels, finish_roots(): pl.pallas_call(functools.partial(root_kernel, groups, owners), out_shape=...  21.3 us
    unnamed x34, local copies, waits for them, and re-layouts  11.6 us
    pallas_call x1, Pallas kernels, prepare(): pl.pallas_call(functools.partial(prepare_kernel, capacity, owners, pieces...  6.72 us
    dot_general x1, matrix products, body(): lax.dot_general(got_tokens, got_signal, (((0,), (0,)), ((), ())), preferr...  4.52 us

profile of v1, /device:TPU:0, one launch (start us, length us, event | category | flops | bytes accessed | tf_op | source)
XLA Modules:
  0.0 139.8 jit_solution(12038315857974595249)
XLA Ops:
  0.6 0.8 copy.9.tall_ref
  1.5 0.0 copy-start.1
  1.5 1.2 copy-done.1
  2.7 0.0 copy-start.5
  2.7 1.2 copy-done.5
  3.9 0.0 copy-start.6
  3.9 1.2 copy-done.6
  5.1 0.0 copy-start.7
  5.1 1.0 copy-done.7
  6.1 0.0 copy-start.9
  6.1 0.7 copy-done.9
  6.8 0.0 copy-start.10
  6.8 0.7 copy-done.10
  7.5 6.7 %shard_map.85 = (bf16[960,1024]{1,0:T(8,128)(2,1)S(1)}, bf16[960,1024]{1,0:T(8,128)(2,1)S(1)}, bf16[256,1024]{1,0:T(8,128)(2,1)S(1)}) custom-call(s32[8]{0:T(128)S(1)} %copy-done.10, s32[480,1]{1,0:T(8,128)S(1)} %copy.9.tall_ref, s32[1,480]{1,0:T(1,128)S(1)} %bitcast.62, bf16[480,1024]{1,0:T(8,128)(2,1)S(1)} %copy-done.5, bf16[480,1024]{1,0:T(8,128)(2,1)S(1)} %copy-done.6, ...), custom_call_target="tpu_custom_call" | custom-call | tf_op jit(solution)/shard_map/pallas_call | solution.py:61
  14.2 0.0 copy-start.3
  14.2 1.3 copy-done.3
  15.5 0.0 copy-start.4
  15.5 1.3 copy-done.4
  16.7 0.0 copy-start.8
  16.7 0.8 copy-done.8
  17.5 48.0 %shard_map.86 = (bf16[8,120,1024]{2,1,0:T(8,128)(2,1)}, bf16[8,120,1024]{2,1,0:T(8,128)(2,1)}, bf16[4,256,1024]{2,1,0:T(8,128)(2,1)}) custom-call(bf16[8,120,1024]{2,1,0:T(8,128)(2,1)} %bitcast.59, bf16[8,120,1024]{2,1,0:T(8,128)(2,1)} %bitcast.60, bf16[256,1024]{1,0:T(8,128)(2,1)} %copy-done.8), custom_call_target="tpu_custom_call" | custom-call | tf_op jit(solution)/shard_map/pallas_call | solution.py:181
  65.5 4.5 %fusion.grad_hbm = bf16[1024,1024]{1,0:T(8,128)(2,1)S(1)} fusion(bf16[8,120,1024]{2,1,0:T(8,128)(2,1)} %get-tuple-element.17, bf16[8,120,1024]{2,1,0:T(8,128)(2,1)} %get-tuple-element.18), kind=kOutput, calls=%fused_computation.1 | convolution fusion | flops 2015363072 | bytes 6029312 | tf_op jit(solution)/shard_map/dot_general | solution.py:472
  70.1 0.5 convolution_convert_fusion.1
  70.5 0.6 fusion.3
  71.1 0.7 convolution_convert_fusion
  71.9 0.0 copy-start
  71.9 0.0 copy-start.2
  72.1 0.4 fusion.7.part_ref
  72.5 1.1 copy-done
  73.5 0.3 copy-done.2
  73.8 0.0 copy-start.11
  73.8 44.5 %shard_map.87 = (bf16[1024,1024]{1,0:T(8,128)(2,1)S(1)}, f32[256,1024]{1,0:T(8,128)S(1)}) custom-call(bf16[10,256,256]{2,1,0:T(8,128)(2,1)S(1)} %fusion.7.part_ref, bf16[4,256,1024]{2,1,0:T(8,128)(2,1)S(1)} %copy-done, f32[256,1024]{1,0:T(8,128)S(1)} %bitcast.58), custom_call_target="tpu_custom_call" | custom-call | tf_op jit(solution)/shard_map/pallas_call | solution.py:326
  118.3 0.0 copy-done.11
  118.4 21.3 %shard_map.88 = (bf16[256,1024]{1,0:T(8,128)(2,1)}, bf16[1024,1024]{1,0:T(8,128)(2,1)}, f32[256,1024]{1,0:T(8,128)}) custom-call(s32[8]{0:T(128)S(1)} %copy-done.11, bf16[1024,1024]{1,0:T(8,128)(2,1)S(1)} %get-tuple-element.20.low_ref, bf16[1024,1024]{1,0:T(8,128)(2,1)S(1)} %bitcast.56, bf16[1024,1024]{1,0:T(8,128)(2,1)S(1)} %fusion.grad_hbm, ...), custom_call_target="tpu_custom_call" | custom-call | tf_op jit(solution)/shard_map/pallas_call | solution.py:435
  (9 shorter events, 0.1 us)
Async XLA Ops:
  1.5 1.2 copy-start.1
  2.7 1.2 copy-start.5
  3.9 1.2 copy-start.6
  5.1 1.0 copy-start.7
  6.1 0.7 copy-start.9
  6.8 0.7 copy-start.10
  14.2 1.3 copy-start.3
  15.5 1.3 copy-start.4
  16.7 0.8 copy-start.8
  71.9 1.6 %copy-start = (bf16[4,256,1024]{2,1,0:T(8,128)(2,1)S(1)}, bf16[4,256,1024]{2,1,0:T(8,128)(2,1)}, u32[]{:S(2)}) copy-start(bf16[4,256,1024]{2,1,0:T(8,128)(2,1)} %get-tuple-element.19.full_ref) | copy-start | bytes 6291460
  71.9 1.8 %copy-start.2 = (f32[1,256,1024]{2,1,0:T(8,128)S(1)}, f32[1,256,1024]{2,1,0:T(8,128)}, u32[]{:S(2)}) copy-start(f32[1,256,1024]{2,1,0:T(8,128)} %param.9) | copy-start | bytes 3145732
  73.8 44.6 %copy-start.11 = (s32[8]{0:T(128)S(1)}, s32[8]{0:T(128)}, u32[]{:S(2)}) copy-start(s32[8]{0:T(128)} %owner_ref.3) | copy-start | bytes 100

commit v2 on v1

--- a/solution.py
+++ b/solution.py
@@ -65,7 +65,6 @@
         out_specs=(anywhere,) * 3,
         scratch_shapes=[pltpu.VMEM(shape, jnp.bfloat16) for shape in shapes]
         + [pltpu.SemaphoreType.DMA((2 * pieces + 1,))],
-        compiler_params=pltpu.CompilerParams(vmem_limit_bytes=40 << 20),
     )(owner_map, routing, routing.reshape(1, -1), tokens, cotangent, prev_rows, old_rows)
 
 
@@ -445,7 +444,6 @@
             pltpu.VMEM(stat.shape, jnp.float32), tall, square, square, square, square, square, tall,
             pltpu.SemaphoreType.DMA((4 + groups,)),
         ],
-        compiler_params=pltpu.CompilerParams(vmem_limit_bytes=40 << 20),
     )(owner_map, low, full, grad, stat)
 
 

time: 140 us -> 134 us (0.957)
  the two profiles are of different devices: /device:TPU:0 before, /device:TPU:4 now
where the time goes in v2:
time: 134 us; the launch traced here: 132 us
  Pallas kernels  119 us (89%)
  matrix products  6.7 us (5%)
  local copies, waits for them, and re-layouts  5.26 us (4%)
    pallas_call x1, Pallas kernels, exchange(): pl.pallas_call(functools.partial(exchange_kernel, experts, groups), out_s...  46.6 us
    pallas_call x1, Pallas kernels, chain_sum(): pl.pallas_call(functools.partial(chain_kernel, groups, share), out_shape=...  43.4 us
    pallas_call x1, Pallas kernels, finish_roots(): pl.pallas_call(functools.partial(root_kernel, groups, owners), out_shape=...  24 us
    pallas_call x1, Pallas kernels, prepare(): pl.pallas_call(functools.partial(prepare_kernel, capacity, owners, pieces...  5.5 us
    unnamed x20, local copies, waits for them, and re-layouts  5.26 us
    dot_general x1, matrix products, body(): lax.dot_general(got_tokens, got_signal, (((0,), (0,)), ((), ())), preferr...  4.52 us

profile of v2, /device:TPU:4, one launch (start us, length us, event | category | flops | bytes accessed | tf_op | source)
XLA Modules:
  0.0 132.4 jit_solution(509767591956576205)
XLA Ops:
  0.6 1.5 %copy.9.tall_ref = s32[480,1]{1,0:T(8,128)} copy(s32[480,1]{0,1:T(1,128)} %param.8) | data formatting | bytes 3840 | tf_op args[2]
  2.1 5.5 %shard_map.85 = (bf16[960,1024]{1,0:T(8,128)(2,1)}, bf16[960,1024]{1,0:T(8,128)(2,1)}, bf16[256,1024]{1,0:T(8,128)(2,1)}) custom-call(s32[8]{0:T(128)} %owner_ref.3, s32[480,1]{1,0:T(8,128)} %copy.9.tall_ref, s32[1,480]{1,0:T(1,128)} %bitcast.62, bf16[480,1024]{1,0:T(8,128)(2,1)} %tok_ref.1, bf16[480,1024]{1,0:T(8,128)(2,1)} %sig_ref.1, ...), custom_call_target="tpu_custom_call" | custom-call | tf_op jit(solution)/shard_map/pallas_call | solution.py:61
  7.7 46.6 %shard_map.86 = (bf16[8,120,1024]{2,1,0:T(8,128)(2,1)}, bf16[8,120,1024]{2,1,0:T(8,128)(2,1)}, bf16[4,256,1024]{2,1,0:T(8,128)(2,1)}) custom-call(bf16[8,120,1024]{2,1,0:T(8,128)(2,1)} %bitcast.59, bf16[8,120,1024]{2,1,0:T(8,128)(2,1)} %bitcast.60, bf16[256,1024]{1,0:T(8,128)(2,1)} %get-tuple-element.16.pay_ref), custom_call_target="tpu_custom_call" | custom-call | tf_op jit(solution)/shard_map/pallas_call | solution.py:180
  54.3 4.5 %fusion.grad_hbm = bf16[1024,1024]{1,0:T(8,128)(2,1)S(1)} fusion(bf16[8,120,1024]{2,1,0:T(8,128)(2,1)} %get-tuple-element.17, bf16[8,120,1024]{2,1,0:T(8,128)(2,1)} %get-tuple-element.18), kind=kOutput, calls=%fused_computation.1 | convolution fusion | flops 2015363072 | bytes 6029312 | tf_op jit(solution)/shard_map/dot_general | solution.py:470
  58.8 0.0 copy-start.4
  58.8 0.5 convolution_convert_fusion.1
  59.3 0.6 fusion.3
  59.9 0.7 convolution_convert_fusion
  60.7 0.0 copy-start
  60.7 0.0 copy-start.1
  60.9 0.0 copy-done.4
  60.9 0.4 fusion.7.part_ref
  61.2 1.0 copy-done
  62.3 0.3 copy-done.1
  62.6 43.4 %shard_map.87 = (bf16[1024,1024]{1,0:T(8,128)(2,1)S(1)}, f32[256,1024]{1,0:T(8,128)S(1)}) custom-call(bf16[10,256,256]{2,1,0:T(8,128)(2,1)S(1)} %fusion.7.part_ref, bf16[4,256,1024]{2,1,0:T(8,128)(2,1)S(1)} %copy-done, f32[256,1024]{1,0:T(8,128)S(1)} %bitcast.58), custom_call_target="tpu_custom_call" | custom-call | tf_op jit(solution)/shard_map/pallas_call | solution.py:325
  106.0 0.0 copy-start.2
  106.0 1.3 copy-done.2
  107.3 0.0 copy-start.3
  107.3 1.0 copy-done.3
  108.3 24.0 %shard_map.88 = (bf16[256,1024]{1,0:T(8,128)(2,1)}, bf16[1024,1024]{1,0:T(8,128)(2,1)}, f32[256,1024]{1,0:T(8,128)}) custom-call(s32[8]{0:T(128)} %owner_ref.3, bf16[1024,1024]{1,0:T(8,128)(2,1)} %copy-done.2, bf16[1024,1024]{1,0:T(8,128)(2,1)} %bitcast.56, bf16[1024,1024]{1,0:T(8,128)(2,1)} %copy-done.4, f32[256,1024]{1,0:T(8,128)} %copy-done.3), custom_call_target="tpu_custom_call" | custom-call | tf_op jit(solution)/shard_map/pallas_call | solution.py:434
  (9 shorter events, 0.1 us)
Async XLA Ops:
  58.8 2.1 %copy-start.4 = (bf16[1024,1024]{1,0:T(8,128)(2,1)}, bf16[1024,1024]{1,0:T(8,128)(2,1)S(1)}, u32[]{:S(2)}) copy-start(bf16[1024,1024]{1,0:T(8,128)(2,1)S(1)} %fusion.grad_hbm) | copy-start | bytes 6291460
  60.7 1.6 %copy-start = (bf16[4,256,1024]{2,1,0:T(8,128)(2,1)S(1)}, bf16[4,256,1024]{2,1,0:T(8,128)(2,1)}, u32[]{:S(2)}) copy-start(bf16[4,256,1024]{2,1,0:T(8,128)(2,1)} %get-tuple-element.19.full_ref) | copy-start | bytes 6291460
  60.7 1.8 %copy-start.1 = (f32[1,256,1024]{2,1,0:T(8,128)S(1)}, f32[1,256,1024]{2,1,0:T(8,128)}, u32[]{:S(2)}) copy-start(f32[1,256,1024]{2,1,0:T(8,128)} %param.9) | copy-start | bytes 3145732
  106.0 1.3 copy-start.2
  107.3 1.0 copy-start.3

commit v3 on v2

--- a/solution.py
+++ b/solution.py
@@ -444,6 +444,7 @@
             pltpu.VMEM(stat.shape, jnp.float32), tall, square, square, square, square, square, tall,
             pltpu.SemaphoreType.DMA((4 + groups,)),
         ],
+        compiler_params=pltpu.CompilerParams(vmem_limit_bytes=40 << 20),
     )(owner_map, low, full, grad, stat)
 
 

time: 134 us -> 129 us (0.963)
  the two profiles are of different devices: /device:TPU:4 before, /device:TPU:2 now
where the time goes in v3:
time: 129 us; the launch traced here: 127 us
  Pallas kernels  117 us (91%)
  matrix products  6.68 us (5%)
  local copies, waits for them, and re-layouts  2.98 us (2%)
    pallas_call x1, Pallas kernels, exchange(): pl.pallas_call(functools.partial(exchange_kernel, experts, groups), out_s...  46.6 us
    pallas_call x1, Pallas kernels, chain_sum(): pl.pallas_call(functools.partial(chain_kernel, groups, share), out_shape=...  43.5 us
    pallas_call x1, Pallas kernels, finish_roots(): pl.pallas_call(functools.partial(root_kernel, groups, owners), out_shape=...  21.3 us
    pallas_call x1, Pallas kernels, prepare(): pl.pallas_call(functools.partial(prepare_kernel, capacity, owners, pieces...  5.51 us
    dot_general x1, matrix products, body(): lax.dot_general(got_tokens, got_signal, (((0,), (0,)), ((), ())), preferr...  4.52 us
    unnamed x16, local copies, waits for them, and re-layouts  2.98 us

profile of v3, /device:TPU:2, one launch (start us, length us, event | category | flops | bytes accessed | tf_op | source)
XLA Modules:
  0.0 127.5 jit_solution(12395371489663855960)
XLA Ops:
  0.6 1.5 %copy.9.tall_ref = s32[480,1]{1,0:T(8,128)} copy(s32[480,1]{0,1:T(1,128)} %param.8) | data formatting | bytes 3840 | tf_op args[2]
  2.1 5.5 %shard_map.85 = (bf16[960,1024]{1,0:T(8,128)(2,1)}, bf16[960,1024]{1,0:T(8,128)(2,1)}, bf16[256,1024]{1,0:T(8,128)(2,1)}) custom-call(s32[8]{0:T(128)} %owner_ref.3, s32[480,1]{1,0:T(8,128)} %copy.9.tall_ref, s32[1,480]{1,0:T(1,128)} %bitcast.62, bf16[480,1024]{1,0:T(8,128)(2,1)} %tok_ref.1, bf16[480,1024]{1,0:T(8,128)(2,1)} %sig_ref.1, ...), custom_call_target="tpu_custom_call" | custom-call | tf_op jit(solution)/shard_map/pallas_call | solution.py:61
  7.7 46.6 %shard_map.86 = (bf16[8,120,1024]{2,1,0:T(8,128)(2,1)}, bf16[8,120,1024]{2,1,0:T(8,128)(2,1)}, bf16[4,256,1024]{2,1,0:T(8,128)(2,1)}) custom-call(bf16[8,120,1024]{2,1,0:T(8,128)(2,1)} %bitcast.59, bf16[8,120,1024]{2,1,0:T(8,128)(2,1)} %bitcast.60, bf16[256,1024]{1,0:T(8,128)(2,1)} %get-tuple-element.16.pay_ref), custom_call_target="tpu_custom_call" | custom-call | tf_op jit(solution)/shard_map/pallas_call | solution.py:180
  54.3 4.5 %fusion.grad_hbm = bf16[1024,1024]{1,0:T(8,128)(2,1)S(1)} fusion(bf16[8,120,1024]{2,1,0:T(8,128)(2,1)} %get-tuple-element.17, bf16[8,120,1024]{2,1,0:T(8,128)(2,1)} %get-tuple-element.18), kind=kOutput, calls=%fused_computation.1 | convolution fusion | flops 2015363072 | bytes 6029312 | tf_op jit(solution)/shard_map/dot_general | solution.py:471
  58.8 0.5 convolution_convert_fusion.1
  59.3 0.6 fusion.3
  59.9 0.7 convolution_convert_fusion
  60.7 0.0 copy-start
  60.7 0.0 copy-start.1
  60.9 0.4 fusion.7.part_ref
  61.2 1.1 copy-done
  62.3 0.3 copy-done.1
  62.6 0.0 copy-start.2
  62.6 43.5 %shard_map.87 = (bf16[1024,1024]{1,0:T(8,128)(2,1)S(1)}, f32[256,1024]{1,0:T(8,128)S(1)}) custom-call(bf16[10,256,256]{2,1,0:T(8,128)(2,1)S(1)} %fusion.7.part_ref, bf16[4,256,1024]{2,1,0:T(8,128)(2,1)S(1)} %copy-done, f32[256,1024]{1,0:T(8,128)S(1)} %bitcast.58), custom_call_target="tpu_custom_call" | custom-call | tf_op jit(solution)/shard_map/pallas_call | solution.py:325
  106.0 0.0 copy-done.2
  106.0 21.3 %shard_map.88 = (bf16[256,1024]{1,0:T(8,128)(2,1)}, bf16[1024,1024]{1,0:T(8,128)(2,1)}, f32[256,1024]{1,0:T(8,128)}) custom-call(s32[8]{0:T(128)S(1)} %copy-done.2, bf16[1024,1024]{1,0:T(8,128)(2,1)S(1)} %get-tuple-element.20.low_ref, bf16[1024,1024]{1,0:T(8,128)(2,1)S(1)} %bitcast.56, bf16[1024,1024]{1,0:T(8,128)(2,1)S(1)} %fusion.grad_hbm, ...), custom_call_target="tpu_custom_call" | custom-call | tf_op jit(solution)/shard_map/pallas_call | solution.py:434
  (9 shorter events, 0.1 us)
Async XLA Ops:
  60.7 1.6 %copy-start = (bf16[4,256,1024]{2,1,0:T(8,128)(2,1)S(1)}, bf16[4,256,1024]{2,1,0:T(8,128)(2,1)}, u32[]{:S(2)}) copy-start(bf16[4,256,1024]{2,1,0:T(8,128)(2,1)} %get-tuple-element.19.full_ref) | copy-start | bytes 6291460
  60.7 1.8 %copy-start.1 = (f32[1,256,1024]{2,1,0:T(8,128)S(1)}, f32[1,256,1024]{2,1,0:T(8,128)}, u32[]{:S(2)}) copy-start(f32[1,256,1024]{2,1,0:T(8,128)} %param.9) | copy-start | bytes 3145732
  62.6 43.5 %copy-start.2 = (s32[8]{0:T(128)S(1)}, s32[8]{0:T(128)}, u32[]{:S(2)}) copy-start(s32[8]{0:T(128)} %owner_ref.3) | copy-start | bytes 100
